TPU v7x, 32 devices: a whole 2x2x4 slice. The times are simulated.
32 devices in a mesh: lat: 8 (over y, x, core), lon: 4 (over z).
Axes of the slice: x: 2, y: 2, z: 4, core: 2. Of those that a mesh axis runs over, the one named last changes fastest.
Arguments:
- adjoint: float32 [8, 8, 256, 512], P(None, None, 'lat', 'lon'), may hold values from -6 to 6
- transport: float32 [6, 8, 256, 512], P(None, None, 'lat', 'lon'), may hold values from 0.03 to 0.14
- cell_weight: float32 [256, 512], P('lat', 'lon'), may hold values from 0.1 to 1
- region_local: int32 [256, 512], P('lat', 'lon'), may hold values from 0 to 255
- tile_regions: int32 [32, 256], replicated, may hold values from 0 to 2047, as said below
- polar_rows: int32 [256], P('lat'), may hold values 0 or 1
- week_index: int32 [1], replicated, may hold values from 0 to 51
- grad_in: bfloat16 [2048, 416], P(('lat', 'lon')), may hold values from -6 to 6
- covariance: bfloat16 [2048, 2048], P(('lat', 'lon')), may hold values from -0.25 to 0.25
Outputs:
- adjoint_out: float32 [8, 8, 256, 512], P(None, None, 'lat', 'lon')
- precond: float32 [2048, 416], P(('lat', 'lon'))
Inputs may be any that keep to these rules, and one draw needn't show every extreme that they name: `tile_regions`: each row holds 256 different region numbers; with per = 8, entries o * per to o * per + per - 1 of a row lie in regions o * 64 to o * 64 + 63, for every o.
All inputs are finite; a program needn't handle non-finite values. No bound on the sum of `polar_rows` on one device may be relied on, other than what follows from the above.
Results may differ from a plain program's by a relative error of at most 0.00066.
Values may be sent and summed in bfloat16 or wider, within the bound.
No kernel may reach another device: no remote copies, remote signals or barrier semaphores. Data moves between devices by JAX's collectives and lax.ppermute only.
A program may use at most 128 MiB of HBM per device.

v0:
```python
import jax
import jax.numpy as jnp
from jax import lax
from jax.sharding import PartitionSpec as P


def extended(x, sides, width):
    for axis, dim in sides:
        size, length = (lax.axis_size(axis), x.shape[dim])
        up = [(i, (i + 1) % size) for i in range(size)]
        down = [(j, i) for i, j in up]
        last = lax.slice_in_dim(x, length - width, length, axis=dim)
        leading = lax.slice_in_dim(x, 0, width, axis=dim)
        before = lax.ppermute(last, axis, up)
        after = lax.ppermute(leading, axis, down)
        x = jnp.concatenate([before, x, after], axis=dim)
    return x


def advance(padded, rates):
    centre = padded[:, :, 1:-1, 1:-1]
    to_east = padded[:, :, 1:-1, 2:] - centre
    to_west = padded[:, :, 1:-1, :-2] - centre
    to_north = padded[:, :, 2:, 1:-1] - centre
    to_south = padded[:, :, :-2, 1:-1] - centre
    flat_zero = jnp.zeros_like(centre[:, :1])
    upper = jnp.concatenate([centre[:, 1:] - centre[:, :-1], flat_zero], axis=1)
    lower = jnp.concatenate([flat_zero, centre[:, :-1] - centre[:, 1:]], axis=1)
    return (
        centre
        + rates[0] * to_east
        + rates[1] * to_west
        + rates[2] * to_north
        + rates[3] * to_south
        + rates[4] * upper
        + rates[5] * lower
    )


def pole_mask(padded, margin, interior):
    band = lax.axis_index("lat")
    last_band = lax.axis_size("lat") - 1
    row_ids = jnp.arange(interior + 2 * margin, dtype=jnp.int32)
    outside = (row_ids < margin) & (band == 0) | (row_ids >= interior + margin) & (
        band == last_band
    )
    return jnp.where(outside[None, None, :, None], 0.0, padded)


def shards(
    adjoint,
    transport,
    cell_weight,
    region_local,
    tile_regions,
    polar_rows,
    week_index,
    grad_in,
    covariance,
):
    tracers, levels, lat_rows, lon_cols = adjoint.shape
    region_count = covariance.shape[1]
    own_rows = covariance.shape[0]
    week_cols = grad_in.shape[1] // tracers
    lon_count = lax.axis_size("lon")
    my_tile = lax.axis_index("lat") * lon_count + lax.axis_index("lon")
    base = jnp.dot(
        covariance,
        lax.all_gather(grad_in, ("lat", "lon"), axis=0, tiled=True),
        preferred_element_type=jnp.float32,
    )
    field = adjoint
    for repeat in range(2):
        padded = extended(field, (("lat", 2), ("lon", 3)), 1)
        field = advance(pole_mask(padded, 1, lat_rows), transport)
    row_sums = lax.psum(jnp.sum(field, axis=3), "lon")
    zonal = row_sums / (lon_cols * lon_count)
    flags = polar_rows.astype(jnp.float32)[None, None, :, None]
    adjoint_out = field + 0.5 * flags * (zonal[..., None] - field)
    surface = (adjoint_out[:, 0] * cell_weight[None]).reshape(tracers, -1)
    local_count = tile_regions.shape[1]
    one_hot = (
        region_local.reshape(1, -1) == jnp.arange(local_count, dtype=jnp.int32)[:, None]
    ).astype(jnp.float32)
    local_sums = lax.dot_general(
        one_hot,
        surface,
        (((1,), (1,)), ((), ())),
        precision=lax.Precision.HIGHEST,
        preferred_element_type=jnp.float32,
    )
    my_regions = lax.dynamic_index_in_dim(tile_regions, my_tile, 0, keepdims=False)
    dense = jnp.zeros((region_count, tracers), jnp.float32).at[my_regions].add(local_sums)
    fresh_all = lax.psum(dense, ("lat", "lon")).astype(jnp.bfloat16)
    added = jnp.dot(covariance, fresh_all, preferred_element_type=jnp.float32)
    week_hot = (jnp.arange(week_cols, dtype=jnp.int32) == week_index[0]).astype(jnp.float32)
    precond = (
        base.reshape(own_rows, week_cols, tracers) + week_hot[None, :, None] * added[:, None, :]
    )
    return (adjoint_out, precond.reshape(own_rows, week_cols * tracers))


def solution(mesh):
    in_specs = (
        P(None, None, "lat", "lon"),
        P(None, None, "lat", "lon"),
        P("lat", "lon"),
        P("lat", "lon"),
        P(),
        P("lat"),
        P(),
        P(("lat", "lon"), None),
        P(("lat", "lon"), None),
    )
    out_specs = (P(None, None, "lat", "lon"), P(("lat", "lon"), None))
    return jax.shard_map(shards, mesh=mesh, in_specs=in_specs, out_specs=out_specs, check_vma=False)
```

profile of v0, /device:TPU:0, one launch (start us, length us, event | category | flops | bytes accessed | tf_op | source)
XLA Modules:
  0.0 179.2 jit_solution(4061105329152444854)
XLA Ops:
  8.9 2.9 %collective-permute-start.1 = (f32[8,8,1,128]{3,1,2,0:T(8,128)S(1)}, f32[8,8,1,128]{3,1,2,0:T(8,128)S(1)}, u32[]{:S(2)}, u32[]{:S(2)}) collective-permute-start(f32[8,8,1,128]{3,1,2,0:T(8,128)S(1)} %bitcast.36), channel_id=1, source_target_pairs={{4,0},{8,4},{12,8},{16,12},{20,16},{24,20},{28,24},{0,28},{5,1},{9... | collective-permute-start | bytes 98312 | tf_op jit(solution)/shard_map/ppermute | solution.py:15
  13.8 3.6 %copy.81 = f32[8,8,32,128]{2,1,3,0:T(8,128)} copy(f32[8,8,32,128]{3,2,1,0:T(8,128)} %param.9) | data formatting | bytes 2097152 | tf_op args[0]
  17.4 2.6 %copy.80 = f32[8,8,1,128]{2,1,3,0:T(8,128)} copy(f32[8,8,1,128]{3,1,2,0:T(8,128)S(1)} %collective-permute-done) | data formatting | bytes 65536 | tf_op jit(solution)/shard_map/ppermute | solution.py:14
  20.1 2.6 %copy.82 = f32[8,8,1,128]{2,1,3,0:T(8,128)} copy(f32[8,8,1,128]{3,1,2,0:T(8,128)S(1)} %collective-permute-done.1) | data formatting | bytes 65536 | tf_op jit(solution)/shard_map/ppermute | solution.py:15
  23.6 2.3 %collective-permute-start.2 = (f32[8,8,34,1]{2,1,3,0:T(8,128)S(1)}, f32[8,8,34,1]{2,1,3,0:T(8,128)S(1)}, u32[]{:S(2)}, u32[]{:S(2)}) collective-permute-start(f32[8,8,34,1]{2,1,3,0:T(8,128)S(1)} %get-tuple-element.16), channel_id=1, source_target_pairs={{0,1},{1,2},{2,3},{3,0},{4,5},{5,6},{6,7},{7,4},{8,9},{9,10},{10,1... | collective-permute-start | bytes 26120 | tf_op jit(solution)/shard_map/ppermute | solution.py:14
  26.0 2.1 %collective-permute-start.3 = (f32[8,8,34,1]{2,1,3,0:T(8,128)S(1)}, f32[8,8,34,1]{2,1,3,0:T(8,128)S(1)}, u32[]{:S(2)}, u32[]{:S(2)}) collective-permute-start(f32[8,8,34,1]{2,1,3,0:T(8,128)S(1)} %get-tuple-element.17), channel_id=1, source_target_pairs={{1,0},{2,1},{3,2},{0,3},{5,4},{6,5},{7,6},{4,7},{9,8},{10,9},{11,1... | collective-permute-start | bytes 26120 | tf_op jit(solution)/shard_map/ppermute | solution.py:15
  33.4 5.8 %maximum_select_fusion = f32[8,8,34,130]{2,1,3,0:T(8,128)S(1)} fusion(f32[8,8,34,1]{2,1,3,0:T(8,128)S(1)} %collective-permute-done.3, f32[8,8,1,128]{2,1,3,0:T(8,128)} %copy.82, f32[8,8,32,128]{2,1,3,0:T(8,128)} %copy.81, f32[8,8,1,128]{2,1,3,0:T(8,128)} %copy.80, f32[8,8,34,1]{2,1,3,0:T(8,128)S(1)} %collective-permute-done.2, pred[34]{0:T(512)(128)(4,1)S(1)} %and_or_fusion), kind=kLoop, calls=%fused_computation.1 | loop fusion | flops 1414400 | bytes 2263074 | tf_op jit(solution)/shard_map/jit(_where)/select_n | solution.py:47
  39.2 2.2 %slice_subtract_fusion.11 = (f32[8,7,32,128]{2,1,3,0:T(8,128)S(1)}, f32[8,7,32,128]{2,1,3,0:T(8,128)S(1)}) fusion(f32[8,8,34,130]{2,1,3,0:T(8,128)S(1)} %maximum_select_fusion), kind=kLoop, calls=%fused_computation.37 | loop fusion | flops 458752 | bytes 3670016 | tf_op jit(solution)/shard_map/sub | solution.py:27
  41.4 6.1 %fusion.13 = f32[8,8,32,128]{2,1,3,0:T(8,128)S(1)} fusion(f32[8,8,34,130]{2,1,3,0:T(8,128)S(1)} %maximum_select_fusion, f32[8,7,32,128]{2,1,3,0:T(8,128)S(1)} %get-tuple-element.21, f32[8,7,32,128]{2,1,3,0:T(8,128)S(1)} %get-tuple-element.20, f32[8,32,128]{1,0,2:T(8,128)} %copy.88, f32[8,32,128]{1,0,2:T(8,128)} %copy.87, f32[8,32,128]{1,0,2:T(8,128)} %copy.86, ...), kind=kLoop, calls=%fused_computation.21 | loop fusion | flops 4194304 | bytes 8912896 | tf_op jit(solution)/shard_map/add | solution.py:30
  47.6 4.6 %fusion.29 = (f32[8,8,1,128]{2,1,3,0:T(8,128)}, f32[8,8,1,128]{2,1,3,0:T(8,128)}) fusion(f32[8,8,32,128]{2,1,3,0:T(8,128)S(1)} %fusion.13), kind=kLoop, calls=%fused_computation.66 | loop fusion | bytes 131072 | tf_op jit(solution)/shard_map/slice | solution.py:12
  52.2 2.8 %copy.89 = f32[8,8,1,128]{3,1,2,0:T(8,128)S(1)} copy(f32[8,8,1,128]{2,1,3,0:T(8,128)} %get-tuple-element.22) | data formatting | bytes 65536 | tf_op jit(solution)/shard_map/slice | solution.py:12
  55.1 2.9 %copy.90 = f32[8,8,1,128]{3,1,2,0:T(8,128)S(1)} copy(f32[8,8,1,128]{2,1,3,0:T(8,128)} %get-tuple-element.23) | data formatting | bytes 65536 | tf_op jit(solution)/shard_map/slice | solution.py:13
  58.0 2.9 %collective-permute-start.5 = (f32[8,8,1,128]{3,1,2,0:T(8,128)S(1)}, f32[8,8,1,128]{3,1,2,0:T(8,128)S(1)}, u32[]{:S(2)}, u32[]{:S(2)}) collective-permute-start(f32[8,8,1,128]{3,1,2,0:T(8,128)S(1)} %copy.90), channel_id=1, source_target_pairs={{4,0},{8,4},{12,8},{16,12},{20,16},{24,20},{28,24},{0,28},{5,1},{9... | collective-permute-start | bytes 98312 | tf_op jit(solution)/shard_map/ppermute | solution.py:15
  62.2 2.7 %copy.91 = f32[8,8,1,128]{2,1,3,0:T(8,128)} copy(f32[8,8,1,128]{3,1,2,0:T(8,128)S(1)} %collective-permute-done.4) | data formatting | bytes 65536 | tf_op jit(solution)/shard_map/ppermute | solution.py:14
  64.9 2.7 %copy.92 = f32[8,8,1,128]{2,1,3,0:T(8,128)} copy(f32[8,8,1,128]{3,1,2,0:T(8,128)S(1)} %collective-permute-done.5) | data formatting | bytes 65536 | tf_op jit(solution)/shard_map/ppermute | solution.py:15
  68.7 3.7 %collective-permute-start.7 = (f32[8,8,34,1]{2,1,3,0:T(8,128)S(1)}, f32[8,8,34,1]{2,1,3,0:T(8,128)S(1)}, u32[]{:S(2)}, u32[]{:S(2)}) collective-permute-start(f32[8,8,34,1]{2,1,3,0:T(8,128)S(1)} %get-tuple-element.15), channel_id=1, source_target_pairs={{1,0},{2,1},{3,2},{0,3},{5,4},{6,5},{7,6},{4,7},{9,8},{10,9},{11,1... | collective-permute-start | bytes 26120 | tf_op jit(solution)/shard_map/ppermute | solution.py:15
  74.3 5.8 %maximum_select_fusion.1 = f32[8,8,34,130]{2,1,3,0:T(8,128)S(1)} fusion(f32[8,8,34,1]{2,1,3,0:T(8,128)S(1)} %collective-permute-done.7, f32[8,8,1,128]{2,1,3,0:T(8,128)} %copy.92, f32[8,8,32,128]{2,1,3,0:T(8,128)} %copy-done.1, f32[8,8,1,128]{2,1,3,0:T(8,128)} %copy.91, f32[8,8,34,1]{2,1,3,0:T(8,128)S(1)} %collective-permute-done.6, ...), kind=kLoop, calls=%fused_computation.2 | loop fusion | flops 1414400 | bytes 2263074 | tf_op jit(solution)/shard_map/jit(_where)/select_n | solution.py:47
  80.2 2.2 %slice_subtract_fusion.9 = (f32[8,7,32,128]{2,1,3,0:T(8,128)S(1)}, f32[8,7,32,128]{2,1,3,0:T(8,128)S(1)}) fusion(f32[8,8,34,130]{2,1,3,0:T(8,128)S(1)} %maximum_select_fusion.1), kind=kLoop, calls=%fused_computation.35 | loop fusion | flops 458752 | bytes 3670016 | tf_op jit(solution)/shard_map/sub | solution.py:27
  82.5 6.0 %fusion.27 = (f32[8,8,32]{2,1,0:T(8,128)S(1)}, f32[8,8,32,128]{2,1,3,0:T(8,128)}) fusion(f32[8,7,32,128]{2,1,3,0:T(8,128)S(1)} %get-tuple-element.19, f32[8,32,128]{1,0,2:T(8,128)S(1)} %copy-done.7, f32[8,7,32,128]{2,1,3,0:T(8,128)S(1)} %get-tuple-element.18, f32[8,32,128]{1,0,2:T(8,128)S(1)} %copy-done.6, f32[8,8,34,130]{2,1,3,0:T(8,128)S(1)} %maximum_select_fusion.1, ...), kind=kLoop, calls=%fused_computation.65 | loop fusion | flops 4454400 | bytes 8921088 | tf_op jit(solution)/shard_map/reduce_sum | solution.py:76
  88.4 19.5 %psum.14 = f32[8,8,32]{2,1,0:T(8,128)S(1)} all-reduce(f32[8,8,32]{2,1,0:T(8,128)S(1)} %get-tuple-element.12), channel_id=1, replica_groups=mesh['lat'=8,'lon'=4] {'lon'}, use_global_device_ids=true, to_apply=%region_1.2 | all-reduce | flops 2048 | bytes 16384 | tf_op jit(solution)/shard_map/psum | solution.py:76
  108.0 2.6 %multiply_add_fusion = f32[8,8,32,128]{2,1,3,0:T(8,128)S(1)} fusion(f32[8,8,32,128]{2,1,3,0:T(8,128)} %get-tuple-element.13, f32[8,8,32]{2,1,0:T(8,128)S(1)} %broadcast_multiply_fusion, f32[32]{0:T(128)S(1)} %convert_multiply_fusion), kind=kLoop, calls=%fused_computation.32 | loop fusion | flops 786432 | bytes 2105472 | tf_op jit(solution)/shard_map/add | solution.py:79
  112.6 3.7 %copy.96 = f32[8,8,32,128]{3,2,1,0:T(8,128)} copy(f32[8,8,32,128]{2,1,3,0:T(8,128)} %copy-done.2) | data formatting | bytes 2097152
  120.1 49.0 %psum.15 = bf16[2048,8]{1,0:T(8,128)(2,1)S(1)} all-reduce(f32[2048,8]{1,0:T(8,128)S(1)} %scatter_custom_fusion), channel_id=1, replica_groups=mesh['lat'=8,'lon'=4] {'lat','lon'}, use_global_device_ids=true, to_apply=%region_3.4 | all-reduce | flops 16384 | bytes 98304 | tf_op jit(solution)/shard_map/psum | solution.py:94
  169.7 2.7 %convolution_add_fusion = f32[64,416]{1,0:T(8,128)} fusion(bf16[64,2048]{1,0:T(8,128)(2,1)S(1)} %copy-done, bf16[2048,416]{1,0:T(8,128)(2,1)} %all-gather.2.cloned.1.call-done, f32[64,416]{1,0:T(8,128)S(1)} %copy.95, f32[416]{0:T(512)S(1)} %mul.174), kind=kOutput, calls=%fused_computation.39 | convolution fusion | flops 109105152 | bytes 2180736 | tf_op jit(solution)/shard_map/dot_general | solution.py:67
  (59 shorter events, 20.0 us)
Async XLA Ops:
  7.2 162.0 %copy-start = (bf16[64,2048]{1,0:T(8,128)(2,1)S(1)}, bf16[64,2048]{1,0:T(8,128)(2,1)}, u32[]{:S(2)}) copy-start(bf16[64,2048]{1,0:T(8,128)(2,1)} %param.17) | copy-start | bytes 786436
  7.2 162.5 %all-gather.2.cloned.1.call-start = ((), (), s32[]{:S(2)}) async-start(), calls=%async_computation | async-start | bytes 2162688 | tf_op jit(solution)/shard_map/all_gather | solution.py:69
  8.3 9.1 %collective-permute-start = (f32[8,8,1,128]{3,1,2,0:T(8,128)S(1)}, f32[8,8,1,128]{3,1,2,0:T(8,128)S(1)}, u32[]{:S(2)}, u32[]{:S(2)}) collective-permute-start(f32[8,8,1,128]{3,1,2,0:T(8,128)S(1)} %bitcast.37), channel_id=1, source_target_pairs={{0,4},{4,8},{8,12},{12,16},{16,20},{20,24},{24,28},{28,0},{1,5},{5... | collective-permute-start | bytes 98312 | tf_op jit(solution)/shard_map/ppermute | solution.py:14
  8.9 11.2 %collective-permute-start.1 = (f32[8,8,1,128]{3,1,2,0:T(8,128)S(1)}, f32[8,8,1,128]{3,1,2,0:T(8,128)S(1)}, u32[]{:S(2)}, u32[]{:S(2)}) collective-permute-start(f32[8,8,1,128]{3,1,2,0:T(8,128)S(1)} %bitcast.36), channel_id=1, source_target_pairs={{4,0},{8,4},{12,8},{16,12},{20,16},{24,20},{28,24},{0,28},{5,1},{9... | collective-permute-start | bytes 98312 | tf_op jit(solution)/shard_map/ppermute | solution.py:15
  23.6 9.7 %collective-permute-start.2 = (f32[8,8,34,1]{2,1,3,0:T(8,128)S(1)}, f32[8,8,34,1]{2,1,3,0:T(8,128)S(1)}, u32[]{:S(2)}, u32[]{:S(2)}) collective-permute-start(f32[8,8,34,1]{2,1,3,0:T(8,128)S(1)} %get-tuple-element.16), channel_id=1, source_target_pairs={{0,1},{1,2},{2,3},{3,0},{4,5},{5,6},{6,7},{7,4},{8,9},{9,10},{10,1... | collective-permute-start | bytes 26120 | tf_op jit(solution)/shard_map/ppermute | solution.py:14
  26.0 7.4 %collective-permute-start.3 = (f32[8,8,34,1]{2,1,3,0:T(8,128)S(1)}, f32[8,8,34,1]{2,1,3,0:T(8,128)S(1)}, u32[]{:S(2)}, u32[]{:S(2)}) collective-permute-start(f32[8,8,34,1]{2,1,3,0:T(8,128)S(1)} %get-tuple-element.17), channel_id=1, source_target_pairs={{1,0},{2,1},{3,2},{0,3},{5,4},{6,5},{7,6},{4,7},{9,8},{10,9},{11,1... | collective-permute-start | bytes 26120 | tf_op jit(solution)/shard_map/ppermute | solution.py:15
  47.6 4.6 %copy-start.1 = (f32[8,8,32,128]{2,1,3,0:T(8,128)}, f32[8,8,32,128]{2,1,3,0:T(8,128)S(1)}, u32[]{:S(2)}) copy-start(f32[8,8,32,128]{2,1,3,0:T(8,128)S(1)} %fusion.13) | copy-start | bytes 3145732
  55.1 7.1 %collective-permute-start.4 = (f32[8,8,1,128]{3,1,2,0:T(8,128)S(1)}, f32[8,8,1,128]{3,1,2,0:T(8,128)S(1)}, u32[]{:S(2)}, u32[]{:S(2)}) collective-permute-start(f32[8,8,1,128]{3,1,2,0:T(8,128)S(1)} %copy.89), channel_id=1, source_target_pairs={{0,4},{4,8},{8,12},{12,16},{16,20},{20,24},{24,28},{28,0},{1,5},{5... | collective-permute-start | bytes 98312 | tf_op jit(solution)/shard_map/ppermute | solution.py:14
  58.0 6.9 %collective-permute-start.5 = (f32[8,8,1,128]{3,1,2,0:T(8,128)S(1)}, f32[8,8,1,128]{3,1,2,0:T(8,128)S(1)}, u32[]{:S(2)}, u32[]{:S(2)}) collective-permute-start(f32[8,8,1,128]{3,1,2,0:T(8,128)S(1)} %copy.90), channel_id=1, source_target_pairs={{4,0},{8,4},{12,8},{16,12},{20,16},{24,20},{28,24},{0,28},{5,1},{9... | collective-permute-start | bytes 98312 | tf_op jit(solution)/shard_map/ppermute | solution.py:15
  68.5 5.8 %collective-permute-start.6 = (f32[8,8,34,1]{2,1,3,0:T(8,128)S(1)}, f32[8,8,34,1]{2,1,3,0:T(8,128)S(1)}, u32[]{:S(2)}, u32[]{:S(2)}) collective-permute-start(f32[8,8,34,1]{2,1,3,0:T(8,128)S(1)} %get-tuple-element.14), channel_id=1, source_target_pairs={{0,1},{1,2},{2,3},{3,0},{4,5},{5,6},{6,7},{7,4},{8,9},{9,10},{10,1... | collective-permute-start | bytes 26120 | tf_op jit(solution)/shard_map/ppermute | solution.py:14
  68.7 5.6 %collective-permute-start.7 = (f32[8,8,34,1]{2,1,3,0:T(8,128)S(1)}, f32[8,8,34,1]{2,1,3,0:T(8,128)S(1)}, u32[]{:S(2)}, u32[]{:S(2)}) collective-permute-start(f32[8,8,34,1]{2,1,3,0:T(8,128)S(1)} %get-tuple-element.15), channel_id=1, source_target_pairs={{1,0},{2,1},{3,2},{0,3},{5,4},{6,5},{7,6},{4,7},{9,8},{10,9},{11,1... | collective-permute-start | bytes 26120 | tf_op jit(solution)/shard_map/ppermute | solution.py:15
  80.1 2.3 %copy-start.3 = (f32[8,32,128]{1,0,2:T(8,128)S(1)}, f32[8,32,128]{1,0,2:T(8,128)}, u32[]{:S(2)}) copy-start(f32[8,32,128]{1,0,2:T(8,128)} %copy.84) | copy-start | bytes 393220
  80.2 2.3 %copy-start.4 = (f32[8,32,128]{1,0,2:T(8,128)S(1)}, f32[8,32,128]{1,0,2:T(8,128)}, u32[]{:S(2)}) copy-start(f32[8,32,128]{1,0,2:T(8,128)} %copy.85) | copy-start | bytes 393220
  80.2 2.3 %copy-start.5 = (f32[8,32,128]{1,0,2:T(8,128)S(1)}, f32[8,32,128]{1,0,2:T(8,128)}, u32[]{:S(2)}) copy-start(f32[8,32,128]{1,0,2:T(8,128)} %copy.86) | copy-start | bytes 393220
  80.2 2.3 %copy-start.6 = (f32[8,32,128]{1,0,2:T(8,128)S(1)}, f32[8,32,128]{1,0,2:T(8,128)}, u32[]{:S(2)}) copy-start(f32[8,32,128]{1,0,2:T(8,128)} %copy.87) | copy-start | bytes 393220
  80.2 2.3 %copy-start.7 = (f32[8,32,128]{1,0,2:T(8,128)S(1)}, f32[8,32,128]{1,0,2:T(8,128)}, u32[]{:S(2)}) copy-start(f32[8,32,128]{1,0,2:T(8,128)} %copy.88) | copy-start | bytes 393220
  110.6 2.0 %copy-start.2 = (f32[8,8,32,128]{2,1,3,0:T(8,128)}, f32[8,8,32,128]{2,1,3,0:T(8,128)S(1)}, u32[]{:S(2)}) copy-start(f32[8,8,32,128]{2,1,3,0:T(8,128)S(1)} %multiply_add_fusion) | copy-start | bytes 3145732
  112.6 3.9 %copy-start.8 = (s32[32,128]{1,0:T(8,128)S(1)}, s32[32,128]{1,0:T(8,128)}, u32[]{:S(2)}) copy-start(s32[32,128]{1,0:T(8,128)} %param.12) | copy-start | bytes 49156
  112.6 3.9 %copy-start.9 = (f32[32,128]{1,0:T(8,128)S(1)}, f32[32,128]{1,0:T(8,128)}, u32[]{:S(2)}) copy-start(f32[32,128]{1,0:T(8,128)} %param.11) | copy-start | bytes 49156
  112.6 3.7 %slice-start = ((f32[8,8,32,128]{2,1,3,0:T(8,128)}), f32[8,1,32,128]{2,1,3,0:T(1,128)S(1)}, s32[]{:S(2)}) async-start(f32[8,8,32,128]{2,1,3,0:T(8,128)} %copy-done.2), calls=%async_computation.1 | async-start | bytes 1048576 | tf_op jit(solution)/shard_map/slice | solution.py:80
Sparse Core Ops, SparseCore 0:
  12.0 58.4 all-gather.1
where the time goes:
time: 180 us; the launch traced here: 179 us
  blocking collectives  68.5 us (38%)
  local copies, waits for them, and re-layouts  38.5 us (21%)
  other arithmetic  35.8 us (20%)
  between operations  15 us (8%)
  starting transfers between devices  14.7 us (8%)
  matrix products  4.95 us (3%)
    psum x1, blocking collectives, shards(): fresh_all = lax.psum(dense, ('lat', 'lon')).astype(jnp.bfloat16)  49 us
    psum x1, blocking collectives, shards(): row_sums = lax.psum(jnp.sum(field, axis=3), 'lon')  19.5 us
    select_n x2, other arithmetic, pole_mask(): return jnp.where(outside[None, None, :, None], 0.0, padded)  11.7 us
    ppermute x4, starting transfers between devices, extended(): after = lax.ppermute(leading, axis, down)  11.6 us
    unnamed x22, local copies, waits for them, and re-layouts  9.28 us
    slice x3, local copies, waits for them, and re-layouts, extended(): last = lax.slice_in_dim(x, length - width, length, axis=dim)  8.58 us
    add x1, other arithmetic, advance(): centre + rates[0] * to_east + rates[1] * to_west + rates[2] * to_north  6.13 us
    reduce_sum x1, other arithmetic, shards(): row_sums = lax.psum(jnp.sum(field, axis=3), 'lon')  5.98 us
  transfers between devices with their start and end apart: 9, of which 1 were waited for; matrix products, arithmetic and copies ran while one was open for 41% of the time, Pallas kernels for 0%

commit v1 on v0

--- a/solution.py
+++ b/solution.py
@@ -91,7 +91,7 @@
     )
     my_regions = lax.dynamic_index_in_dim(tile_regions, my_tile, 0, keepdims=False)
     dense = jnp.zeros((region_count, tracers), jnp.float32).at[my_regions].add(local_sums)
-    fresh_all = lax.psum(dense, ("lat", "lon")).astype(jnp.bfloat16)
+    fresh_all = lax.psum(lax.psum(dense, "lon"), "lat").astype(jnp.bfloat16)
     added = jnp.dot(covariance, fresh_all, preferred_element_type=jnp.float32)
     week_hot = (jnp.arange(week_cols, dtype=jnp.int32) == week_index[0]).astype(jnp.float32)
     precond = (

time: 180 us -> 231 us (1.28)
  waiting for transfers between devices: 1.77 us -> 49.8 us
  blocking collectives: 68.5 us -> 73.5 us
  other arithmetic: 35.8 us -> 32.6 us
    psum x0 -> x1, waiting for transfers between devices: none -> 48.1 us  [shards(): fresh_all = lax.psum(lax.psum(dense, 'lon'), 'lat').astype(jnp.bfloat16)]
    psum x1, blocking collectives: 49 us -> 54 us  [shards(): fresh_all = lax.psum(lax.psum(dense, 'lon'), 'lat').astype(jnp.bfloat16)]
    select_n x2, other arithmetic: 11.7 us -> 8.19 us  [pole_mask(): return jnp.where(outside[None, None, :, None], 0.0, padded)]
    unnamed x22 -> x30, local copies, waits for them, and re-layouts: 9.28 us -> 9.44 us
  transfers between devices with their start and end apart: 9 -> 10, of which waited for: 1 -> 2; matrix products, arithmetic and copies ran while one was open for 41% -> 10% of each run, Pallas kernels for 0% -> 0%
where the time goes in v1:
time: 231 us
  blocking collectives  73.5 us (32%)
  waiting for transfers between devices  49.8 us (22%)
  local copies, waits for them, and re-layouts  38.9 us (17%)
  other arithmetic  32.6 us (14%)
  between operations  16.5 us (7%)
  starting transfers between devices  14.7 us (6%)
  matrix products  4.95 us (2%)
    psum x1, blocking collectives, shards(): fresh_all = lax.psum(lax.psum(dense, 'lon'), 'lat').astype(jnp.bfloat16)  54 us
    psum x1, waiting for transfers between devices, shards(): fresh_all = lax.psum(lax.psum(dense, 'lon'), 'lat').astype(jnp.bfloat16)  48.1 us
    psum x1, blocking collectives, shards(): row_sums = lax.psum(jnp.sum(field, axis=3), 'lon')  19.5 us
    ppermute x4, starting transfers between devices, extended(): after = lax.ppermute(leading, axis, down)  11.7 us
    unnamed x30, local copies, waits for them, and re-layouts  9.44 us
    slice x3, local copies, waits for them, and re-layouts, extended(): last = lax.slice_in_dim(x, length - width, length, axis=dim)  8.59 us
    select_n x2, other arithmetic, pole_mask(): return jnp.where(outside[None, None, :, None], 0.0, padded)  8.19 us
    add x1, other arithmetic, advance(): centre + rates[0] * to_east + rates[1] * to_west + rates[2] * to_north  6.13 us
  transfers between devices with their start and end apart: 10, of which 2 were waited for; matrix products, arithmetic and copies ran while one was open for 10% of the time, Pallas kernels for 0%

profile of v1, /device:TPU:0, one launch (start us, length us, event | category | flops | bytes accessed | tf_op | source)
XLA Modules:
  0.0 231.0 jit_solution(6755786671100585919)
XLA Ops:
  9.7 2.9 %collective-permute-start.1 = (f32[8,8,1,128]{3,1,2,0:T(8,128)S(1)}, f32[8,8,1,128]{3,1,2,0:T(8,128)S(1)}, u32[]{:S(2)}, u32[]{:S(2)}) collective-permute-start(f32[8,8,1,128]{3,1,2,0:T(8,128)S(1)} %bitcast.36), channel_id=1, source_target_pairs={{4,0},{8,4},{12,8},{16,12},{20,16},{24,20},{28,24},{0,28},{5,1},{9... | collective-permute-start | bytes 98312 | tf_op jit(solution)/shard_map/ppermute | solution.py:15
  13.9 3.7 %copy.81 = f32[8,8,32,128]{2,1,3,0:T(8,128)} copy(f32[8,8,32,128]{3,2,1,0:T(8,128)} %param.9) | data formatting | bytes 2097152 | tf_op args[0]
  17.6 2.6 %copy.80 = f32[8,8,1,128]{2,1,3,0:T(8,128)} copy(f32[8,8,1,128]{3,1,2,0:T(8,128)S(1)} %collective-permute-done) | data formatting | bytes 65536 | tf_op jit(solution)/shard_map/ppermute | solution.py:14
  20.2 2.6 %copy.82 = f32[8,8,1,128]{2,1,3,0:T(8,128)} copy(f32[8,8,1,128]{3,1,2,0:T(8,128)S(1)} %collective-permute-done.1) | data formatting | bytes 65536 | tf_op jit(solution)/shard_map/ppermute | solution.py:15
  23.8 2.3 %collective-permute-start.2 = (f32[8,8,34,1]{2,1,3,0:T(8,128)S(1)}, f32[8,8,34,1]{2,1,3,0:T(8,128)S(1)}, u32[]{:S(2)}, u32[]{:S(2)}) collective-permute-start(f32[8,8,34,1]{2,1,3,0:T(8,128)S(1)} %get-tuple-element.16), channel_id=1, source_target_pairs={{0,1},{1,2},{2,3},{3,0},{4,5},{5,6},{6,7},{7,4},{8,9},{9,10},{10,1... | collective-permute-start | bytes 26120 | tf_op jit(solution)/shard_map/ppermute | solution.py:14
  33.5 5.8 %maximum_select_fusion = f32[8,8,34,130]{2,1,3,0:T(8,128)S(1)} fusion(f32[8,8,34,1]{2,1,3,0:T(8,128)S(1)} %collective-permute-done.3, f32[8,8,1,128]{2,1,3,0:T(8,128)} %copy.82, f32[8,8,32,128]{2,1,3,0:T(8,128)} %copy.81, f32[8,8,1,128]{2,1,3,0:T(8,128)} %copy.80, f32[8,8,34,1]{2,1,3,0:T(8,128)S(1)} %collective-permute-done.2, pred[34]{0:T(512)(128)(4,1)S(1)} %and_or_fusion), kind=kLoop, calls=%fused_computation.1 | loop fusion | flops 1414400 | bytes 2263074 | tf_op jit(solution)/shard_map/jit(_where)/select_n | solution.py:47
  39.4 2.2 slice_subtract_fusion.11
  41.6 6.1 %fusion.13 = f32[8,8,32,128]{2,1,3,0:T(8,128)S(1)} fusion(f32[8,8,34,130]{2,1,3,0:T(8,128)S(1)} %maximum_select_fusion, f32[8,7,32,128]{2,1,3,0:T(8,128)S(1)} %get-tuple-element.21, f32[8,7,32,128]{2,1,3,0:T(8,128)S(1)} %get-tuple-element.20, f32[8,32,128]{1,0,2:T(8,128)} %copy.88, f32[8,32,128]{1,0,2:T(8,128)} %copy.87, f32[8,32,128]{1,0,2:T(8,128)} %copy.86, ...), kind=kLoop, calls=%fused_computation.21 | loop fusion | flops 4194304 | bytes 8912896 | tf_op jit(solution)/shard_map/add | solution.py:30
  47.7 4.6 %fusion.29 = (f32[8,8,1,128]{2,1,3,0:T(8,128)}, f32[8,8,1,128]{2,1,3,0:T(8,128)}) fusion(f32[8,8,32,128]{2,1,3,0:T(8,128)S(1)} %fusion.13), kind=kLoop, calls=%fused_computation.66 | loop fusion | bytes 131072 | tf_op jit(solution)/shard_map/slice | solution.py:12
  52.4 2.9 %copy.89 = f32[8,8,1,128]{3,1,2,0:T(8,128)S(1)} copy(f32[8,8,1,128]{2,1,3,0:T(8,128)} %get-tuple-element.22) | data formatting | bytes 65536 | tf_op jit(solution)/shard_map/slice | solution.py:12
  55.3 2.9 %copy.90 = f32[8,8,1,128]{3,1,2,0:T(8,128)S(1)} copy(f32[8,8,1,128]{2,1,3,0:T(8,128)} %get-tuple-element.23) | data formatting | bytes 65536 | tf_op jit(solution)/shard_map/slice | solution.py:13
  58.1 2.9 %collective-permute-start.5 = (f32[8,8,1,128]{3,1,2,0:T(8,128)S(1)}, f32[8,8,1,128]{3,1,2,0:T(8,128)S(1)}, u32[]{:S(2)}, u32[]{:S(2)}) collective-permute-start(f32[8,8,1,128]{3,1,2,0:T(8,128)S(1)} %copy.90), channel_id=1, source_target_pairs={{4,0},{8,4},{12,8},{16,12},{20,16},{24,20},{28,24},{0,28},{5,1},{9... | collective-permute-start | bytes 98312 | tf_op jit(solution)/shard_map/ppermute | solution.py:15
  61.0 2.7 %copy.91 = f32[8,8,1,128]{2,1,3,0:T(8,128)} copy(f32[8,8,1,128]{3,1,2,0:T(8,128)S(1)} %collective-permute-done.4) | data formatting | bytes 65536 | tf_op jit(solution)/shard_map/ppermute | solution.py:14
  63.7 2.7 %copy.92 = f32[8,8,1,128]{2,1,3,0:T(8,128)} copy(f32[8,8,1,128]{3,1,2,0:T(8,128)S(1)} %collective-permute-done.5) | data formatting | bytes 65536 | tf_op jit(solution)/shard_map/ppermute | solution.py:15
  67.5 3.8 %collective-permute-start.7 = (f32[8,8,34,1]{2,1,3,0:T(8,128)S(1)}, f32[8,8,34,1]{2,1,3,0:T(8,128)S(1)}, u32[]{:S(2)}, u32[]{:S(2)}) collective-permute-start(f32[8,8,34,1]{2,1,3,0:T(8,128)S(1)} %get-tuple-element.15), channel_id=1, source_target_pairs={{1,0},{2,1},{3,2},{0,3},{5,4},{6,5},{7,6},{4,7},{9,8},{10,9},{11,1... | collective-permute-start | bytes 26120 | tf_op jit(solution)/shard_map/ppermute | solution.py:15
  73.2 2.3 %maximum_select_fusion.1 = f32[8,8,34,130]{2,1,3,0:T(8,128)S(1)} fusion(f32[8,8,34,1]{2,1,3,0:T(8,128)S(1)} %collective-permute-done.7, f32[8,8,1,128]{2,1,3,0:T(8,128)S(1)} %copy-done.4, f32[8,8,32,128]{2,1,3,0:T(8,128)S(1)} %copy-done.2, f32[8,8,1,128]{2,1,3,0:T(8,128)S(1)} %copy-done.3, f32[8,8,34,1]{2,1,3,0:T(8,128)S(1)} %collective-permute-done.6, ...), kind=kLoop, calls=%fused_computation.2 | loop fusion | flops 1414400 | bytes 2263074 | tf_op jit(solution)/shard_map/jit(_where)/select_n | solution.py:47
  77.9 6.0 %fusion.27 = (f32[8,8,32]{2,1,0:T(8,128)S(1)}, f32[8,8,32,128]{2,1,3,0:T(8,128)}) fusion(f32[8,7,32,128]{2,1,3,0:T(8,128)S(1)} %get-tuple-element.19, f32[8,32,128]{1,0,2:T(8,128)S(1)} %copy-done.10, f32[8,7,32,128]{2,1,3,0:T(8,128)S(1)} %get-tuple-element.18, f32[8,32,128]{1,0,2:T(8,128)S(1)} %copy-done.9, f32[8,8,34,130]{2,1,3,0:T(8,128)S(1)} %maximum_select_fusion.1, ...), kind=kLoop, calls=%fused_computation.65 | loop fusion | flops 4454400 | bytes 8921088 | tf_op jit(solution)/shard_map/reduce_sum | solution.py:76
  83.9 19.5 %psum.21 = f32[8,8,32]{2,1,0:T(8,128)S(1)} all-reduce(f32[8,8,32]{2,1,0:T(8,128)S(1)} %get-tuple-element.12), channel_id=1, replica_groups=mesh['lat'=8,'lon'=4] {'lon'}, use_global_device_ids=true, to_apply=%region_1.2 | all-reduce | flops 2048 | bytes 16384 | tf_op jit(solution)/shard_map/psum | solution.py:76
  103.4 2.6 %multiply_add_fusion = f32[8,8,32,128]{2,1,3,0:T(8,128)S(1)} fusion(f32[8,8,32,128]{2,1,3,0:T(8,128)} %get-tuple-element.13, f32[8,8,32]{2,1,0:T(8,128)S(1)} %broadcast_multiply_fusion, f32[32]{0:T(128)S(1)} %convert_multiply_fusion), kind=kLoop, calls=%fused_computation.32 | loop fusion | flops 786432 | bytes 2105472 | tf_op jit(solution)/shard_map/add | solution.py:79
  110.5 2.5 %scatter_custom_fusion = f32[2048,8]{1,0:T(8,128)} fusion(s32[256]{0:T(256)S(1)} %bitcast.38, f32[256,8]{1,0:T(8,128)S(1)} %fusion.20, f32[]{:T(128)} %constant.8.clone.1), kind=kCustom, calls=%fused_computation.42 | custom fusion | flops 2048 | bytes 65540 | tf_op jit(solution)/shard_map/scatter-add | solution.py:93
  114.4 3.8 %copy.96 = f32[8,8,32,128]{3,2,1,0:T(8,128)} copy(f32[8,8,32,128]{2,1,3,0:T(8,128)} %copy-done.5) | data formatting | bytes 2097152
  118.2 48.1 %all-reduce.6.cloned.1.call-done = f32[2048,8]{1,0:T(8,128)} async-done(((f32[2048,8]{1,0:T(8,128)}), f32[2048,8]{1,0:T(8,128)}) %all-reduce.6.cloned.1.call-update) | async-done | bytes 65552 | tf_op jit(solution)/shard_map/psum | solution.py:94
  166.3 54.0 %psum.23 = bf16[2048,8]{1,0:T(8,128)(2,1)S(1)} all-reduce(f32[2048,8]{1,0:T(8,128)} %all-reduce.6.cloned.1.call-done), channel_id=1, replica_groups=mesh['lat'=8,'lon'=4] {'lat'}, use_global_device_ids=true, to_apply=%region_4.5 | all-reduce | flops 16384 | bytes 98304 | tf_op jit(solution)/shard_map/psum | solution.py:94
  220.8 2.7 %convolution_add_fusion = f32[64,416]{1,0:T(8,128)} fusion(bf16[64,2048]{1,0:T(8,128)(2,1)S(1)} %copy-done, bf16[2048,416]{1,0:T(8,128)(2,1)} %all-gather.2.cloned.1.call-done, f32[64,416]{1,0:T(8,128)S(1)} %copy.95, f32[416]{0:T(512)S(1)} %mul.174), kind=kOutput, calls=%fused_computation.39 | convolution fusion | flops 109105152 | bytes 2180736 | tf_op jit(solution)/shard_map/dot_general | solution.py:67
  (69 shorter events, 22.3 us)
Async XLA Ops:
  8.0 212.3 %copy-start = (bf16[64,2048]{1,0:T(8,128)(2,1)S(1)}, bf16[64,2048]{1,0:T(8,128)(2,1)}, u32[]{:S(2)}) copy-start(bf16[64,2048]{1,0:T(8,128)(2,1)} %param.17) | copy-start | bytes 786436
  8.0 158.3 %all-reduce.6.cloned.1.call-start = ((), (), s32[]{:S(2)}) async-start(), calls=%async_computation.1 | async-start | bytes 2097152 | tf_op jit(solution)/shard_map/psum | solution.py:94
  9.2 8.4 %collective-permute-start = (f32[8,8,1,128]{3,1,2,0:T(8,128)S(1)}, f32[8,8,1,128]{3,1,2,0:T(8,128)S(1)}, u32[]{:S(2)}, u32[]{:S(2)}) collective-permute-start(f32[8,8,1,128]{3,1,2,0:T(8,128)S(1)} %bitcast.37), channel_id=1, source_target_pairs={{0,4},{4,8},{8,12},{12,16},{16,20},{20,24},{24,28},{28,0},{1,5},{5... | collective-permute-start | bytes 98312 | tf_op jit(solution)/shard_map/ppermute | solution.py:14
  9.7 10.5 %collective-permute-start.1 = (f32[8,8,1,128]{3,1,2,0:T(8,128)S(1)}, f32[8,8,1,128]{3,1,2,0:T(8,128)S(1)}, u32[]{:S(2)}, u32[]{:S(2)}) collective-permute-start(f32[8,8,1,128]{3,1,2,0:T(8,128)S(1)} %bitcast.36), channel_id=1, source_target_pairs={{4,0},{8,4},{12,8},{16,12},{20,16},{24,20},{28,24},{0,28},{5,1},{9... | collective-permute-start | bytes 98312 | tf_op jit(solution)/shard_map/ppermute | solution.py:15
  23.8 9.8 %collective-permute-start.2 = (f32[8,8,34,1]{2,1,3,0:T(8,128)S(1)}, f32[8,8,34,1]{2,1,3,0:T(8,128)S(1)}, u32[]{:S(2)}, u32[]{:S(2)}) collective-permute-start(f32[8,8,34,1]{2,1,3,0:T(8,128)S(1)} %get-tuple-element.16), channel_id=1, source_target_pairs={{0,1},{1,2},{2,3},{3,0},{4,5},{5,6},{6,7},{7,4},{8,9},{9,10},{10,1... | collective-permute-start | bytes 26120 | tf_op jit(solution)/shard_map/ppermute | solution.py:14
  26.1 7.4 %collective-permute-start.3 = (f32[8,8,34,1]{2,1,3,0:T(8,128)S(1)}, f32[8,8,34,1]{2,1,3,0:T(8,128)S(1)}, u32[]{:S(2)}, u32[]{:S(2)}) collective-permute-start(f32[8,8,34,1]{2,1,3,0:T(8,128)S(1)} %get-tuple-element.17), channel_id=1, source_target_pairs={{1,0},{2,1},{3,2},{0,3},{5,4},{6,5},{7,6},{4,7},{9,8},{10,9},{11,1... | collective-permute-start | bytes 26120 | tf_op jit(solution)/shard_map/ppermute | solution.py:15
  47.7 4.6 %copy-start.1 = (f32[8,8,32,128]{2,1,3,0:T(8,128)}, f32[8,8,32,128]{2,1,3,0:T(8,128)S(1)}, u32[]{:S(2)}) copy-start(f32[8,8,32,128]{2,1,3,0:T(8,128)S(1)} %fusion.13) | copy-start | bytes 3145732
  52.4 8.6 %copy-start.13 = (s32[32]{0:T(128)S(1)}, s32[32]{0:T(128)}, u32[]{:S(2)}) copy-start(s32[32]{0:T(128)} %param.14) | copy-start | bytes 388
  55.2 5.8 %collective-permute-start.4 = (f32[8,8,1,128]{3,1,2,0:T(8,128)S(1)}, f32[8,8,1,128]{3,1,2,0:T(8,128)S(1)}, u32[]{:S(2)}, u32[]{:S(2)}) collective-permute-start(f32[8,8,1,128]{3,1,2,0:T(8,128)S(1)} %copy.89), channel_id=1, source_target_pairs={{0,4},{4,8},{8,12},{12,16},{16,20},{20,24},{24,28},{28,0},{1,5},{5... | collective-permute-start | bytes 98312 | tf_op jit(solution)/shard_map/ppermute | solution.py:14
  58.1 5.5 %collective-permute-start.5 = (f32[8,8,1,128]{3,1,2,0:T(8,128)S(1)}, f32[8,8,1,128]{3,1,2,0:T(8,128)S(1)}, u32[]{:S(2)}, u32[]{:S(2)}) collective-permute-start(f32[8,8,1,128]{3,1,2,0:T(8,128)S(1)} %copy.90), channel_id=1, source_target_pairs={{4,0},{8,4},{12,8},{16,12},{20,16},{24,20},{28,24},{0,28},{5,1},{9... | collective-permute-start | bytes 98312 | tf_op jit(solution)/shard_map/ppermute | solution.py:15
  66.3 6.9 %copy-start.2 = (f32[8,8,32,128]{2,1,3,0:T(8,128)S(1)}, f32[8,8,32,128]{2,1,3,0:T(8,128)}, u32[]{:S(2)}) copy-start(f32[8,8,32,128]{2,1,3,0:T(8,128)} %copy-done.1) | copy-start | bytes 3145732
  66.3 6.9 %copy-start.3 = (f32[8,8,1,128]{2,1,3,0:T(8,128)S(1)}, f32[8,8,1,128]{2,1,3,0:T(8,128)}, u32[]{:S(2)}) copy-start(f32[8,8,1,128]{2,1,3,0:T(8,128)} %copy.91) | copy-start | bytes 98308
  66.3 6.9 %copy-start.4 = (f32[8,8,1,128]{2,1,3,0:T(8,128)S(1)}, f32[8,8,1,128]{2,1,3,0:T(8,128)}, u32[]{:S(2)}) copy-start(f32[8,8,1,128]{2,1,3,0:T(8,128)} %copy.92) | copy-start | bytes 98308
  67.4 5.8 %collective-permute-start.6 = (f32[8,8,34,1]{2,1,3,0:T(8,128)S(1)}, f32[8,8,34,1]{2,1,3,0:T(8,128)S(1)}, u32[]{:S(2)}, u32[]{:S(2)}) collective-permute-start(f32[8,8,34,1]{2,1,3,0:T(8,128)S(1)} %get-tuple-element.14), channel_id=1, source_target_pairs={{0,1},{1,2},{2,3},{3,0},{4,5},{5,6},{6,7},{7,4},{8,9},{9,10},{10,1... | collective-permute-start | bytes 26120 | tf_op jit(solution)/shard_map/ppermute | solution.py:14
  67.5 5.7 %collective-permute-start.7 = (f32[8,8,34,1]{2,1,3,0:T(8,128)S(1)}, f32[8,8,34,1]{2,1,3,0:T(8,128)S(1)}, u32[]{:S(2)}, u32[]{:S(2)}) collective-permute-start(f32[8,8,34,1]{2,1,3,0:T(8,128)S(1)} %get-tuple-element.15), channel_id=1, source_target_pairs={{1,0},{2,1},{3,2},{0,3},{5,4},{6,5},{7,6},{4,7},{9,8},{10,9},{11,1... | collective-permute-start | bytes 26120 | tf_op jit(solution)/shard_map/ppermute | solution.py:15
  75.6 2.3 copy-start.6
  75.6 2.3 copy-start.7
  75.6 2.3 copy-start.8
  75.6 2.3 copy-start.9
  75.6 2.3 copy-start.10
  103.4 5.2 %copy-start.11 = (s32[32,128]{1,0:T(8,128)S(1)}, s32[32,128]{1,0:T(8,128)}, u32[]{:S(2)}) copy-start(s32[32,128]{1,0:T(8,128)} %param.12) | copy-start | bytes 49156
  103.4 5.2 %copy-start.12 = (f32[32,128]{1,0:T(8,128)S(1)}, f32[32,128]{1,0:T(8,128)}, u32[]{:S(2)}) copy-start(f32[32,128]{1,0:T(8,128)} %param.11) | copy-start | bytes 49156
  106.0 1.9 copy-start.5
  113.0 107.8 %all-gather.2.cloned.1.call-start = ((), (), s32[]{:S(2)}) async-start(), calls=%async_computation | async-start | bytes 2162688 | tf_op jit(solution)/shard_map/all_gather | solution.py:69
Sparse Core Ops, SparseCore 0:
  113.2 53.0 all-reduce.5
Sparse Core Ops, SparseCore 1:
  116.5 69.1 all-gather.1
